TPU v7x, 32 devices: a whole 2x2x4 slice. The times are simulated.
32 devices in a mesh: grp: 1, ep: 32 (over z, y, x, core).
Axes of the slice: x: 2, y: 2, z: 4, core: 2. Of those that a mesh axis runs over, the one named last changes fastest.
Arguments:
- hidden_states: bfloat16 [192, 3584], P(('grp', 'ep')), may hold values from -6 to 6
- norm_gain: float32 [3584], replicated, may hold values from 0.1 to 1.9
- gate_scores: float32 [192, 8], P(('grp', 'ep')), may hold values from 0.05 to 1
- routes: int32 [192, 8], P(('grp', 'ep')), may hold values from 0 to 15, all different within a row; in each aligned block of 6 rows (0 to 5, 6 to 11, ...) at most 6 rows name the same one
- draft_counts: int32 [64], P(('grp', 'ep')), may hold values from 1 to 2
- w_gate: bfloat16 [32, 3584, 512], P('ep'), may hold values from -0.09375 to 0.09375
- w_up: bfloat16 [32, 3584, 512], P('ep'), may hold values from -0.09375 to 0.09375
- w_down: bfloat16 [32, 512, 3584], P('ep'), may hold values from -0.1875 to 0.1875
Outputs:
- moe_out: bfloat16 [192, 3584], P(('grp', 'ep'))
Inputs may be any that keep to these rules, and one draw needn't show every extreme that they name: `routes`: each token slot names 8 different experts; among the 6 token slots of one device no expert is named more than 6 times.
All inputs are finite; a program needn't handle non-finite values.
Results may differ from a plain program's by a relative error of at most 0.0077.
Values may be sent and summed in bfloat16 or wider, within the bound.
No kernel may reach another device: no remote copies, remote signals or barrier semaphores. Data moves between devices by JAX's collectives and lax.ppermute only.
A program may use at most 64 MiB of HBM per device.

v0:
```python
import jax
import jax.numpy as jnp
from jax import lax
from jax.sharding import PartitionSpec as P


def swapped(array, axis, distance):
    return lax.ppermute(array, axis, [(i, i ^ 1 << distance) for i in range(lax.axis_size(axis))])


def expert_half(received_block, gate_half, up_half, down_half):
    gate_proj = jnp.einsum(
        "ncd,df->ncf", received_block, gate_half[0], preferred_element_type=jnp.float32
    )
    up_proj = jnp.einsum(
        "ncd,df->ncf", received_block, up_half[0], preferred_element_type=jnp.float32
    )
    hidden = (jax.nn.silu(gate_proj) * up_proj).astype(jnp.bfloat16)
    return jnp.einsum(
        "ncf,fd->ncd", hidden, down_half[0], preferred_element_type=jnp.float32
    ).astype(jnp.bfloat16)


def body(hidden_states, norm_gain, gate_scores, routes, draft_counts, w_gate, w_up, w_down):
    token_count, model_width = hidden_states.shape
    top_count = routes.shape[1]
    row_count = draft_counts.shape[0]
    slot_count = token_count // row_count
    devices = lax.axis_size("ep")
    experts = devices // 2
    capacity = min(token_count, 2 * ((token_count * top_count + experts - 1) // experts))
    position = jnp.arange(token_count) % slot_count
    live_mask = (position <= jnp.repeat(draft_counts, slot_count)).astype(jnp.int32)
    wide_states = hidden_states.astype(jnp.float32)
    mean_square = jnp.mean(wide_states * wide_states, axis=-1, keepdims=True)
    normed = (wide_states * lax.rsqrt(mean_square + 1e-06) * norm_gain).astype(jnp.bfloat16)
    gate_weights = 2.5 * gate_scores / jnp.sum(gate_scores, axis=-1, keepdims=True)
    flat_ids = routes.reshape(-1)
    live_entry = jnp.repeat(live_mask, top_count)
    onehot = (flat_ids[:, None] == jnp.arange(experts)[None, :]).astype(jnp.int32) * live_entry[
        :, None
    ]
    slot_rank = jnp.sum(jnp.cumsum(onehot, axis=0) * onehot, axis=1) - 1
    target = flat_ids * capacity + slot_rank
    slot_table = (
        (target[:, None] == jnp.arange(experts * capacity)[None, :]) & (live_entry[:, None] > 0)
    ).astype(jnp.float32)
    per_token = slot_table.reshape(token_count, top_count, experts * capacity)
    dispatch_matrix = jnp.sum(per_token, axis=1).astype(jnp.bfloat16)
    combine_matrix = jnp.sum(per_token * gate_weights[:, :, None], axis=1)
    buffer = jnp.dot(dispatch_matrix.T, normed, preferred_element_type=jnp.float32).astype(
        jnp.bfloat16
    )
    buffer = buffer.reshape(experts, capacity, model_width)
    half_slots = capacity // 2
    outgoing = buffer.reshape(devices, half_slots, model_width)
    own_rows = lax.all_to_all(outgoing, "ep", split_axis=0, concat_axis=0, tiled=True)
    partner = swapped(own_rows, "ep", 0)
    parity = lax.axis_index("ep") % 2
    assembled = jnp.where(
        parity == 0,
        jnp.concatenate([own_rows, partner], axis=1),
        jnp.concatenate([partner, own_rows], axis=1),
    )
    partial_out = expert_half(assembled, gate_half=w_gate, up_half=w_up, down_half=w_down)
    lower_half = partial_out[:, :half_slots]
    upper_half = partial_out[:, half_slots:]
    kept_half = jnp.where(parity == 0, lower_half, upper_half)
    given_half = jnp.where(parity == 0, upper_half, lower_half)
    received = swapped(given_half, "ep", 0)
    summed = (kept_half.astype(jnp.float32) + received.astype(jnp.float32)).astype(jnp.bfloat16)
    returned = lax.all_to_all(summed, "ep", split_axis=0, concat_axis=0, tiled=True)
    expert_out = returned.reshape(experts, capacity, model_width)
    output = jnp.dot(
        combine_matrix,
        expert_out.reshape(experts * capacity, model_width).astype(jnp.float32),
        precision=lax.Precision.HIGHEST,
        preferred_element_type=jnp.float32,
    )
    return output.astype(jnp.bfloat16)


def solution(mesh):
    return jax.shard_map(
        body,
        mesh=mesh,
        in_specs=(
            P(("grp", "ep"), None),
            P(),
            P(("grp", "ep"), None),
            P(("grp", "ep"), None),
            P(("grp", "ep")),
            P("ep", None, None),
            P("ep", None, None),
            P("ep", None, None),
        ),
        out_specs=P(("grp", "ep"), None),
        check_vma=False,
    )
```

profile of v0, /device:TPU:0, one launch (start us, length us, event | category | flops | bytes accessed | tf_op | source)
XLA Modules:
  0.0 81.1 jit_solution(9824850146907269353)
XLA Ops:
  0.0 0.8 eq.38
  0.8 1.0 %fusion.16 = f32[6]{0:T(128)S(1)} fusion(bf16[6,3584]{1,0:T(8,128)(2,1)} %param.8), kind=kLoop, calls=%fused_computation.17 | loop fusion | flops 64506 | bytes 43032 | tf_op jit(solution)/shard_map/reduce_sum | solution.py:35
  1.7 0.7 broadcast_in_dim.4
  2.6 0.8 reduce_sum.46
  3.4 0.8 multiply_divide_fusion
  4.4 0.2 multiply_reduce_fusion
  4.7 0.7 multiply_add_fusion
  5.5 1.2 %convolution_convert_fusion.1 = bf16[96,3584]{1,0:T(8,128)(2,1)S(1)} fusion(bf16[6,3584]{1,0:T(8,128)(2,1)} %param.8, f32[3584]{0:T(1024)} %param.9, f32[6]{0:T(128)S(1)} %add_rsqrt_fusion, bf16[6,96]{1,0:T(8,128)(2,1)S(1)} %get-tuple-element.5), kind=kOutput, calls=%fused_computation.1 | convolution fusion | flops 4558848 | bytes 746648 | tf_op jit(solution)/shard_map/dot_general | solution.py:51
  6.7 0.4 reshape_reshape.6
  7.2 30.5 %all_to_all.10 = bf16[32,3,3584]{2,1,0:T(4,128)(2,1)S(1)} all-to-all(bf16[32,3,3584]{2,1,0:T(4,128)(2,1)S(1)} %reshape_reshape.6), channel_id=1, replica_groups=mesh['grp'=1,'ep'=32] {'ep'}, dimensions={0} | all-to-all | bytes 1376256 | tf_op jit(solution)/shard_map/all_to_all | solution.py:57
  37.7 0.1 copy.18
  37.9 2.1 %collective-permute-done = bf16[32,3,3584]{2,0,1:T(8,128)(2,1)S(1)} collective-permute-done((bf16[32,3,3584]{2,0,1:T(8,128)(2,1)S(1)}, bf16[32,3,3584]{2,0,1:T(8,128)(2,1)S(1)}, u32[]{:S(2)}, u32[]{:S(2)}) %collective-permute-start) | collective-permute-done | bytes 688160 | tf_op jit(solution)/shard_map/ppermute | solution.py:8
  40.1 0.6 copy.19
  40.7 1.6 %maximum_select_fusion = bf16[32,6,3584]{2,1,0:T(8,128)(2,1)S(1)} fusion(bf16[32,3,3584]{2,1,0:T(4,128)(2,1)S(1)} %copy.19, bf16[32,3,3584]{2,1,0:T(4,128)(2,1)S(1)} %all_to_all.10, pred[]{:T(512)S(6)} %eq.45), kind=kLoop, calls=%fused_computation.8 | loop fusion | flops 6193152 | bytes 2752513 | tf_op jit(solution)/shard_map/jit(_where)/select_n | solution.py:60
  42.3 0.4 copy-done
  42.7 1.7 %fusion.1 = f32[32,6,512]{2,0,1:T(8,128)} fusion(bf16[1,3584,512]{2,1,0:T(8,128)(2,1)S(1)} %copy-done, bf16[32,6,3584]{2,1,0:T(8,128)(2,1)S(1)} %maximum_select_fusion), kind=kOutput, calls=%fused_computation.4 | convolution fusion | flops 704643072 | bytes 5439488 | tf_op jit(solution)/shard_map/ncd,df->ncf/dot_general | solution.py:15
  44.4 5.1 %convolution_convert_fusion = bf16[32,6,3584]{2,0,1:T(8,128)(2,1)S(1)} fusion(bf16[1,512,3584]{2,1,0:T(8,128)(2,1)} %param.15, f32[32,6,512]{2,0,1:T(8,128)} %fusion.1, bf16[1,3584,512]{2,1,0:T(8,128)(2,1)} %param.13, bf16[32,6,3584]{2,1,0:T(8,128)(2,1)S(1)} %maximum_select_fusion), kind=kOutput, calls=%fused_computation | convolution fusion | flops 1410564096 | bytes 10485760 | tf_op jit(solution)/shard_map/ncf,fd->ncd/dot_general | solution.py:19
  49.5 0.2 collective-permute-start.1
  49.8 2.0 %collective-permute-done.1 = bf16[32,3,3584]{2,0,1:T(8,128)(2,1)S(1)} collective-permute-done((bf16[32,3,3584]{2,0,1:T(8,128)(2,1)S(1)}, bf16[32,3,3584]{2,0,1:T(8,128)(2,1)S(1)}, u32[]{:S(2)}, u32[]{:S(2)}) %collective-permute-start.1) | collective-permute-done | bytes 688160 | tf_op jit(solution)/shard_map/ppermute | solution.py:8
  51.8 0.2 add_convert_fusion
  52.0 0.6 copy.23
  52.6 26.8 %all_to_all.11 = bf16[32,3,3584]{2,1,0:T(4,128)(2,1)S(1)} all-to-all(bf16[32,3,3584]{2,1,0:T(4,128)(2,1)S(1)} %copy.23), channel_id=1, replica_groups=mesh['grp'=1,'ep'=32] {'ep'}, dimensions={0} | all-to-all | bytes 1376256 | tf_op jit(solution)/shard_map/all_to_all | solution.py:72
  79.4 0.6 reshape_reshape.7
  80.1 1.0 %convolution_convert_fusion.2 = bf16[6,3584]{1,0:T(8,128)(2,1)} fusion(f32[6,96]{1,0:T(8,128)S(1)} %get-tuple-element.6, bf16[96,3584]{1,0:T(8,128)(2,1)S(1)} %reshape_reshape.7), kind=kOutput, calls=%fused_computation.2 | convolution fusion | flops 24794112 | bytes 733440 | tf_op jit(solution)/shard_map/dot_general | solution.py:74
  (13 shorter events, 0.7 us)
Async XLA Ops:
  37.8 2.2 %collective-permute-start = (bf16[32,3,3584]{2,0,1:T(8,128)(2,1)S(1)}, bf16[32,3,3584]{2,0,1:T(8,128)(2,1)S(1)}, u32[]{:S(2)}, u32[]{:S(2)}) collective-permute-start(bf16[32,3,3584]{2,0,1:T(8,128)(2,1)S(1)} %copy.18), channel_id=1, source_target_pairs={{0,1},{1,0},{2,3},{3,2},{4,5},{5,4},{6,7},{7,6},{8,9},{9,8},{10,11... | collective-permute-start | bytes 2064392 | tf_op jit(solution)/shard_map/ppermute | solution.py:8
  40.6 2.0 %copy-start = (bf16[1,3584,512]{2,1,0:T(8,128)(2,1)S(1)}, bf16[1,3584,512]{2,1,0:T(8,128)(2,1)}, u32[]{:S(2)}) copy-start(bf16[1,3584,512]{2,1,0:T(8,128)(2,1)} %param.14) | copy-start | bytes 11010052
  49.5 2.2 %collective-permute-start.1 = (bf16[32,3,3584]{2,0,1:T(8,128)(2,1)S(1)}, bf16[32,3,3584]{2,0,1:T(8,128)(2,1)S(1)}, u32[]{:S(2)}, u32[]{:S(2)}) collective-permute-start(bf16[32,3,3584]{2,0,1:T(8,128)(2,1)S(1)} %broadcast_select_fusion), channel_id=1, source_target_pairs={{0,1},{1,0},{2,3},{3,2},{4,5},{5,4},{6,7},{7,6},{8,9},{9,8},{10,11... | collective-permute-start | bytes 2064392 | tf_op jit(solution)/shard_map/ppermute | solution.py:8
where the time goes:
time: 81.5 us; the launch traced here: 81.1 us
  blocking collectives  57.4 us (70%)
  matrix products  8.99 us (11%)
  other arithmetic  5.62 us (7%)
  local copies, waits for them, and re-layouts  4.57 us (6%)
  waiting for transfers between devices  4.12 us (5%)
    all_to_all x1, blocking collectives, body(): lax.all_to_all(outgoing, 'ep', split_axis=0, concat_axis=0, tiled=True)  30.5 us
    all_to_all x1, blocking collectives, body(): lax.all_to_all(summed, 'ep', split_axis=0, concat_axis=0, tiled=True)  26.8 us
    dot_general x1, matrix products, expert_half(): jnp.einsum('ncf,fd->ncd', hidden, down_half[0], preferred_element_type=jn...  5.1 us
    ppermute x2, waiting for transfers between devices, swapped(): lax.ppermute(array, axis, [(i, i ^ 1 << distance) for i in range(lax.axis...  4.12 us
    dot_general x1, matrix products, expert_half(): jnp.einsum('ncd,df->ncf', received_block, up_half[0], preferred_element_t...  1.67 us
  transfers between devices with their start and end apart: 2, of which 2 were waited for; matrix products, arithmetic and copies ran while one was open for 0% of the time, Pallas kernels for 0%

commit v1 on v0

v1 whole, which is shorter than its diff:
```python
import jax
import jax.numpy as jnp
from jax import lax
from jax.experimental import pallas as pl
from jax.experimental.pallas import tpu as pltpu
from jax.sharding import PartitionSpec as P

VMEM = pl.BlockSpec(memory_space=pltpu.VMEM)
SMEM = pl.BlockSpec(memory_space=pltpu.SMEM)
MIB = 1024 * 1024


def swapped(array, distance):
    size = lax.axis_size("ep")
    return lax.ppermute(array, "ep", [(i, i ^ distance) for i in range(size)])


def lane_round(count):
    return -(-count // 128) * 128


def call(kernel, outs, limit, *args, specs=None, flops=0):
    moved = sum(a.size * a.dtype.itemsize for a in (*args, *outs))
    single = len(outs) == 1
    return pl.pallas_call(
        kernel,
        out_shape=outs[0] if single else tuple(outs),
        in_specs=specs or [VMEM] * len(args),
        out_specs=VMEM if single else tuple([VMEM] * len(outs)),
        compiler_params=pltpu.CompilerParams(vmem_limit_bytes=limit),
        cost_estimate=pl.CostEstimate(flops=flops, bytes_accessed=moved, transcendentals=0),
    )(*args)


def pack_kernel(draft_ref, states_ref, gain_ref, scores_ref, routes_ref, out_ref):
    tokens, width = states_ref.shape
    half = width // 2
    extra = out_ref.shape[2] - half
    requests = draft_ref.shape[0]
    slots = tokens // requests
    wide = states_ref[...].astype(jnp.float32)
    mean_square = jnp.mean(wide * wide, axis=-1, keepdims=True)
    normed = (wide * lax.rsqrt(mean_square + 1e-06) * gain_ref[...]).astype(jnp.bfloat16)
    scores = scores_ref[...]
    weights = 2.5 * scores / jnp.sum(scores, axis=-1, keepdims=True)
    row = lax.broadcasted_iota(jnp.int32, (tokens, 1), 0)
    live = jnp.zeros((tokens, 1), jnp.bool_)
    for request in range(requests):
        inside = (row >= request * slots) & (row <= request * slots + draft_ref[request])
        live = live | (inside & (row < (request + 1) * slots))
    weights = jnp.where(live, weights, 0.0)
    lane = lax.broadcasted_iota(jnp.int32, (tokens, extra), 1)
    coefficient = jnp.zeros((tokens, extra), jnp.float32)
    for k in range(routes_ref.shape[1]):
        coefficient += jnp.where(routes_ref[:, k : k + 1] == lane, weights[:, k : k + 1], 0.0)
    coarse = coefficient.astype(jnp.bfloat16)
    fine = (coefficient - coarse.astype(jnp.float32)).astype(jnp.bfloat16)
    out_ref[0, :, :half] = normed[:, :half]
    out_ref[1, :, :half] = normed[:, half:]
    out_ref[0, :, half:] = coarse
    out_ref[1, :, half:] = fine


def spread_kernel(own_ref, other_ref, out_ref):
    pieces = [own_ref[0], other_ref[0], own_ref[1], other_ref[1]]
    rows = jnp.concatenate([p.astype(jnp.float32) for p in pieces], axis=0).astype(jnp.bfloat16)
    for j in range(out_ref.shape[0]):
        out_ref[j] = rows


def expert_kernel(
    expert_ref, own_ref, other_ref, gate_ref, up_ref, down_ref, keep_ref, give_ref
):
    half = gate_ref.shape[1] // 2
    count = own_ref.shape[1] // 2
    rows = own_ref.shape[0] * count

    def gathered(part):
        pieces = []
        for ref in (own_ref, other_ref):
            for j in range(ref.shape[0]):
                pieces.append(ref[j, part * count : (part + 1) * count, :].astype(jnp.float32))
        return jnp.concatenate(pieces, axis=0)

    low, high = gathered(0), gathered(1)
    mixed = low[:, half:] + high[:, half:]
    lane = lax.broadcasted_iota(jnp.int32, mixed.shape, 1)
    coefficient = jnp.sum(jnp.where(lane == expert_ref[0], mixed, 0.0), axis=1, keepdims=True)
    low = low[:, :half].astype(jnp.bfloat16)
    high = high[:, :half].astype(jnp.bfloat16)

    def projected(ref):
        first = jnp.dot(low, ref[0, :half], preferred_element_type=jnp.float32)
        return first + jnp.dot(high, ref[0, half:], preferred_element_type=jnp.float32)

    gate = projected(gate_ref)
    up = projected(up_ref)
    hidden = (gate / (1.0 + jnp.exp(-gate)) * up).astype(jnp.bfloat16)
    step = down_ref.shape[2] // 7
    for start in range(0, down_ref.shape[2], step):
        columns = slice(start, start + step)
        partial = jnp.dot(hidden, down_ref[0, :, columns], preferred_element_type=jnp.float32)
        partial = partial * coefficient
        keep_ref[:, columns] = partial[:rows]
        give_ref[:, columns] = partial[rows:].astype(jnp.bfloat16)


def fold_kernel(keep_ref, other_ref, out_ref):
    half = keep_ref.shape[1] // 2
    count = out_ref.shape[1] // 2
    for j in range(out_ref.shape[0]):
        rows = slice(j * count, (j + 1) * count)
        total = keep_ref[rows, :] + other_ref[rows, :].astype(jnp.float32)
        both = jnp.concatenate([total[:, :half], total[:, half:]], axis=0)
        out_ref[j] = both.astype(jnp.bfloat16)


def sum_kernel(parts_ref, keep_ref, give_ref):
    half = keep_ref.shape[1] // 2
    tokens = keep_ref.shape[0]
    total = parts_ref[0].astype(jnp.float32)
    for j in range(1, parts_ref.shape[0]):
        total += parts_ref[j].astype(jnp.float32)
    keep_ref[:, :half] = total[:tokens]
    keep_ref[:, half:] = total[2 * tokens : 3 * tokens]
    give_ref[:, :half] = total[tokens : 2 * tokens].astype(jnp.bfloat16)
    give_ref[:, half:] = total[3 * tokens :].astype(jnp.bfloat16)


def finish_kernel(keep_ref, other_ref, out_ref):
    out_ref[...] = (keep_ref[...] + other_ref[...].astype(jnp.float32)).astype(jnp.bfloat16)


def body(hidden_states, norm_gain, gate_scores, routes, draft_counts, w_gate, w_up, w_down):
    tokens, width = hidden_states.shape
    devices = lax.axis_size("ep")
    members = devices // 4
    far = devices // 2
    groups = [
        [2 * m + core + side * far for m in range(members)] for side in range(2) for core in range(2)
    ]
    half = width // 2
    carried = half + lane_round(devices // 2)
    shape = jax.ShapeDtypeStruct
    bf16, f32 = jnp.bfloat16, jnp.float32
    packed = call(
        pack_kernel,
        [shape((2, tokens, carried), bf16)],
        2 * MIB,
        draft_counts,
        hidden_states,
        norm_gain.reshape(1, width),
        gate_scores,
        routes,
        specs=[SMEM] + [VMEM] * 4,
    )
    spread = call(
        spread_kernel,
        [shape((members, 4 * tokens, carried), bf16)],
        8 * MIB,
        packed,
        swapped(packed, far),
    )

    def exchanged(array):
        return lax.all_to_all(
            array, "ep", split_axis=0, concat_axis=0, axis_index_groups=groups, tiled=True
        )

    own = exchanged(spread)
    other = swapped(own, 1)
    rows = members * 2 * tokens
    expert = (lax.axis_index("ep") // 2).astype(jnp.int32).reshape(1)
    keep, give = call(
        expert_kernel,
        [shape((rows, width), f32), shape((rows, width), bf16)],
        48 * MIB,
        expert,
        own,
        other,
        w_gate,
        w_up,
        w_down,
        specs=[SMEM] + [VMEM] * 5,
        flops=12 * rows * width * w_gate.shape[2],
    )
    folded = call(
        fold_kernel,
        [shape((members, 4 * tokens, half), bf16)],
        20 * MIB,
        keep,
        swapped(give, 1),
    )
    keep, give = call(
        sum_kernel,
        [shape((tokens, width), f32), shape((tokens, width), bf16)],
        8 * MIB,
        exchanged(folded),
    )
    return call(
        finish_kernel, [shape((tokens, width), bf16)], 2 * MIB, keep, swapped(give, far)
    )


def solution(mesh):
    return jax.shard_map(
        body,
        mesh=mesh,
        in_specs=(
            P(("grp", "ep"), None),
            P(),
            P(("grp", "ep"), None),
            P(("grp", "ep"), None),
            P(("grp", "ep")),
            P("ep", None, None),
            P("ep", None, None),
            P("ep", None, None),
        ),
        out_specs=P(("grp", "ep"), None),
        check_vma=False,
    )
```

time: 81.5 us -> 60 us (0.74)
  blocking collectives: 57.4 us -> 29.2 us
  matrix products: 8.99 us -> 0 us
  Pallas kernels: 0 us -> 8.38 us
  starting transfers between devices: 0.28 us -> 8.6 us
  waiting for transfers between devices: 4.12 us -> 9.86 us
  other arithmetic: 5.62 us -> 0 us
  local copies, waits for them, and re-layouts: 4.57 us -> 3.57 us
    all_to_all x2, blocking collectives: 57.4 us -> 29.2 us  [exchanged(): lax.all_to_all(array, 'ep', split_axis=0, concat_axis=0, axis_index_group...]
    dot_general x4 -> x0, matrix products: 8.99 us -> none  [the longest x1 5.1 us: expert_half(): jnp.einsum('ncf,fd->ncd', hidden, down_half[0], preferred_element_type=jn...]
    pallas_call x0 -> x6, Pallas kernels: none -> 8.38 us  [call(): pl.pallas_call(kernel, out_shape=outs[0] if single else tuple(outs), in_s...]
    ppermute x2 -> x4, starting transfers between devices: 0.28 us -> 8.6 us  [swapped(): return lax.ppermute(array, 'ep', [(i, i ^ distance) for i in range(size)])]
    ppermute x2 -> x4, waiting for transfers between devices: 4.12 us -> 9.86 us  [swapped(): return lax.ppermute(array, 'ep', [(i, i ^ distance) for i in range(size)])]
    unnamed x2 -> x8, local copies, waits for them, and re-layouts: 0.43 us -> 2.84 us
    reduce_sum x4 -> x0, other arithmetic: 2.05 us -> none  [the longest x1 0.96 us: body(): mean_square = jnp.mean(wide_states * wide_states, axis=-1, keepdims=True)]
    select_n x2 -> x0, other arithmetic: 1.67 us -> none  [the longest x1 1.6 us: body(): jnp.where(parity == 0, jnp.concatenate([own_rows, partner], axis=1), jnp....]
  transfers between devices with their start and end apart: 2 -> 4, of which waited for: 2 -> 4; matrix products, arithmetic and copies ran while one was open for 0% -> 0% of each run, Pallas kernels for 0% -> 0%
where the time goes in v1:
time: 60 us; the launch traced here: 59.6 us
  blocking collectives  29.2 us (49%)
  waiting for transfers between devices  9.86 us (16%)
  starting transfers between devices  8.6 us (14%)
  Pallas kernels  8.38 us (14%)
  local copies, waits for them, and re-layouts  3.57 us (6%)
    all_to_all x2, blocking collectives, exchanged(): lax.all_to_all(array, 'ep', split_axis=0, concat_axis=0, axis_index_group...  29.2 us
    ppermute x4, waiting for transfers between devices, swapped(): return lax.ppermute(array, 'ep', [(i, i ^ distance) for i in range(size)])  9.86 us
    ppermute x4, starting transfers between devices, swapped(): return lax.ppermute(array, 'ep', [(i, i ^ distance) for i in range(size)])  8.6 us
    pallas_call x6, Pallas kernels, call(): pl.pallas_call(kernel, out_shape=outs[0] if single else tuple(outs), in_s...  8.38 us
    unnamed x8, local copies, waits for them, and re-layouts  2.84 us
  transfers between devices with their start and end apart: 4, of which 4 were waited for; matrix products, arithmetic and copies ran while one was open for 0% of the time, Pallas kernels for 0%

profile of v1, /device:TPU:0, one launch (start us, length us, event | category | flops | bytes accessed | tf_op | source)
XLA Modules:
  0.0 59.6 jit_solution(3286253849568541057)
XLA Ops:
  0.0 0.7 %reshape.7.gain_ref = f32[1,3584]{1,0:T(1,128)S(1)} reshape(f32[3584]{0:T(1024)} %param.9) | data formatting | bytes 28672 | tf_op jit(solution)/shard_map/reshape | solution.py:152
  0.7 0.0 copy-start
  0.7 0.8 %copy-done = bf16[6,3584]{1,0:T(8,128)(2,1)S(1)} copy-done((bf16[6,3584]{1,0:T(8,128)(2,1)S(1)}, bf16[6,3584]{1,0:T(8,128)(2,1)}, u32[]{:S(2)}) %copy-start) | copy-done | bytes 43032
  1.6 0.0 copy-start.1
  1.6 0.7 %copy-done.1 = f32[6,8]{1,0:T(8,128)S(1)} copy-done((f32[6,8]{1,0:T(8,128)S(1)}, f32[6,8]{1,0:T(8,128)}, u32[]{:S(2)}) %copy-start.1) | copy-done | bytes 216
  2.2 0.0 copy-start.2
  2.2 0.7 %copy-done.2 = s32[6,8]{1,0:T(8,128)S(1)} copy-done((s32[6,8]{1,0:T(8,128)S(1)}, s32[6,8]{1,0:T(8,128)}, u32[]{:S(2)}) %copy-start.2) | copy-done | bytes 216
  2.9 0.7 %copy-done.3 = s32[2]{0:T(128)S(1)} copy-done((s32[2]{0:T(128)S(1)}, s32[2]{0:T(128)}, u32[]{:S(2)}) %copy-start.3) | copy-done | bytes 32
  3.6 0.7 %shard_map.82.own_ref = bf16[2,6,1920]{2,1,0:T(8,128)(2,1)S(1)} custom-call(s32[2]{0:T(128)S(1)} %copy-done.3, bf16[6,3584]{1,0:T(8,128)(2,1)S(1)} %copy-done, f32[1,3584]{1,0:T(1,128)S(1)} %reshape.7.gain_ref, f32[6,8]{1,0:T(8,128)S(1)} %copy-done.1, s32[6,8]{1,0:T(8,128)S(1)} %copy-done.2), custom_call_target="tpu_custom_call" | custom-call | bytes 103816 | tf_op jit(solution)/shard_map/pallas_call | solution.py:25
  4.3 4.1 %collective-permute-start = (bf16[2,6,1920]{2,1,0:T(8,128)(2,1)S(1)}, bf16[2,6,1920]{2,1,0:T(8,128)(2,1)S(1)}, u32[]{:S(2)}, u32[]{:S(2)}) collective-permute-start(bf16[2,6,1920]{2,1,0:T(8,128)(2,1)S(1)} %shard_map.82.own_ref), channel_id=1, source_target_pairs={{0,16},{1,17},{2,18},{3,19},{4,20},{5,21},{6,22},{7,23},{8,24},{9,... | collective-permute-start | bytes 138248 | tf_op jit(solution)/shard_map/ppermute | solution.py:15
  8.4 2.9 %collective-permute-done.other_ref = bf16[2,6,1920]{2,1,0:T(8,128)(2,1)S(1)} collective-permute-done((bf16[2,6,1920]{2,1,0:T(8,128)(2,1)S(1)}, bf16[2,6,1920]{2,1,0:T(8,128)(2,1)S(1)}, u32[]{:S(2)}, u32[]{:S(2)}) %collective-permute-start) | collective-permute-done | bytes 46112 | tf_op jit(solution)/shard_map/ppermute | solution.py:15
  11.3 0.1 shard_map.83
  11.4 14.9 %all_to_all.10.own_ref = bf16[8,24,1920]{2,1,0:T(8,128)(2,1)S(1)} all-to-all(bf16[8,24,1920]{2,1,0:T(8,128)(2,1)S(1)} %shard_map.83), channel_id=1, replica_groups={{0,2,4,6,8,10,12,14},{1,3,5,7,9,11,13,15},{16,18,20,22,24,26,28,30},{17..., dimensions={0} | all-to-all | bytes 1474560 | tf_op jit(solution)/shard_map/all_to_all | solution.py:166
  26.2 0.0 collective-permute-start.1
  26.2 2.2 %collective-permute-done.1.other_ref = bf16[8,24,1920]{2,1,0:T(8,128)(2,1)S(1)} collective-permute-done((bf16[8,24,1920]{2,1,0:T(8,128)(2,1)S(1)}, bf16[8,24,1920]{2,1,0:T(8,128)(2,1)S(1)}, u32[]{:S(2)}, u32[]{:S(2)}) %collective-permute-start.1) | collective-permute-done | bytes 737312 | tf_op jit(solution)/shard_map/ppermute | solution.py:15
  28.5 6.6 %shard_map.84 = (f32[96,3584]{1,0:T(8,128)S(1)}, bf16[96,3584]{1,0:T(8,128)(2,1)S(1)}) custom-call(s32[1]{0:T(128)} %bitcast.expert_ref, bf16[8,24,1920]{2,1,0:T(8,128)(2,1)S(1)} %all_to_all.10.own_ref, bf16[8,24,1920]{2,1,0:T(8,128)(2,1)S(1)} %collective-permute-done.1.other_ref, bf16[1,3584,512]{2,1,0:T(8,128)(2,1)} %gate_ref.1, ...), custom_call_target="tpu_custom_call" | custom-call | flops 2113929216 | bytes 14548996 | tf_op jit(solution)/shard_map/pallas_call | solution.py:25
  35.1 0.2 collective-permute-start.2
  35.3 2.0 %collective-permute-done.2.other_ref = bf16[96,3584]{1,0:T(8,128)(2,1)S(1)} collective-permute-done((bf16[96,3584]{1,0:T(8,128)(2,1)S(1)}, bf16[96,3584]{1,0:T(8,128)(2,1)S(1)}, u32[]{:S(2)}, u32[]{:S(2)}) %collective-permute-start.2) | collective-permute-done | bytes 688160 | tf_op jit(solution)/shard_map/ppermute | solution.py:15
  37.3 0.2 shard_map.85
  37.5 14.3 %all_to_all.11.parts_ref = bf16[8,24,1792]{2,1,0:T(8,128)(2,1)S(1)} all-to-all(bf16[8,24,1792]{2,1,0:T(8,128)(2,1)S(1)} %shard_map.85), channel_id=1, replica_groups={{0,2,4,6,8,10,12,14},{1,3,5,7,9,11,13,15},{16,18,20,22,24,26,28,30},{17..., dimensions={0} | all-to-all | bytes 1376256 | tf_op jit(solution)/shard_map/all_to_all | solution.py:166
  51.8 0.1 shard_map.86
  51.9 4.3 %collective-permute-start.3 = (bf16[6,3584]{1,0:T(8,128)(2,1)S(1)}, bf16[6,3584]{1,0:T(8,128)(2,1)S(1)}, u32[]{:S(2)}, u32[]{:S(2)}) collective-permute-start(bf16[6,3584]{1,0:T(8,128)(2,1)S(1)} %get-tuple-element.12), channel_id=1, source_target_pairs={{0,16},{1,17},{2,18},{3,19},{4,20},{5,21},{6,22},{7,23},{8,24},{9,... | collective-permute-start | bytes 129032 | tf_op jit(solution)/shard_map/ppermute | solution.py:15
  56.2 2.8 %collective-permute-done.3.other_ref = bf16[6,3584]{1,0:T(8,128)(2,1)S(1)} collective-permute-done((bf16[6,3584]{1,0:T(8,128)(2,1)S(1)}, bf16[6,3584]{1,0:T(8,128)(2,1)S(1)}, u32[]{:S(2)}, u32[]{:S(2)}) %collective-permute-start.3) | collective-permute-done | bytes 43040 | tf_op jit(solution)/shard_map/ppermute | solution.py:15
  59.0 0.6 %shard_map.87 = bf16[6,3584]{1,0:T(8,128)(2,1)} custom-call(f32[6,3584]{1,0:T(8,128)S(1)} %get-tuple-element.11.keep_ref, bf16[6,3584]{1,0:T(8,128)(2,1)S(1)} %collective-permute-done.3.other_ref), custom_call_target="tpu_custom_call" | custom-call | bytes 172032 | tf_op jit(solution)/shard_map/pallas_call | solution.py:25
  (1 shorter events, 0.0 us)
Async XLA Ops:
  0.7 0.8 %copy-start = (bf16[6,3584]{1,0:T(8,128)(2,1)S(1)}, bf16[6,3584]{1,0:T(8,128)(2,1)}, u32[]{:S(2)}) copy-start(bf16[6,3584]{1,0:T(8,128)(2,1)} %states_ref.1) | copy-start | bytes 129028
  1.6 0.7 %copy-start.1 = (f32[6,8]{1,0:T(8,128)S(1)}, f32[6,8]{1,0:T(8,128)}, u32[]{:S(2)}) copy-start(f32[6,8]{1,0:T(8,128)} %scores_ref.1) | copy-start | bytes 580
  2.2 0.7 %copy-start.2 = (s32[6,8]{1,0:T(8,128)S(1)}, s32[6,8]{1,0:T(8,128)}, u32[]{:S(2)}) copy-start(s32[6,8]{1,0:T(8,128)} %routes_ref.1) | copy-start | bytes 580
  2.9 0.7 %copy-start.3 = (s32[2]{0:T(128)S(1)}, s32[2]{0:T(128)}, u32[]{:S(2)}) copy-start(s32[2]{0:T(128)} %draft_ref.1) | copy-start | bytes 28
  4.3 7.0 %collective-permute-start = (bf16[2,6,1920]{2,1,0:T(8,128)(2,1)S(1)}, bf16[2,6,1920]{2,1,0:T(8,128)(2,1)S(1)}, u32[]{:S(2)}, u32[]{:S(2)}) collective-permute-start(bf16[2,6,1920]{2,1,0:T(8,128)(2,1)S(1)} %shard_map.82.own_ref), channel_id=1, source_target_pairs={{0,16},{1,17},{2,18},{3,19},{4,20},{5,21},{6,22},{7,23},{8,24},{9,... | collective-permute-start | bytes 138248 | tf_op jit(solution)/shard_map/ppermute | solution.py:15
  26.2 2.2 %collective-permute-start.1 = (bf16[8,24,1920]{2,1,0:T(8,128)(2,1)S(1)}, bf16[8,24,1920]{2,1,0:T(8,128)(2,1)S(1)}, u32[]{:S(2)}, u32[]{:S(2)}) collective-permute-start(bf16[8,24,1920]{2,1,0:T(8,128)(2,1)S(1)} %all_to_all.10.own_ref), channel_id=1, source_target_pairs={{0,1},{1,0},{2,3},{3,2},{4,5},{5,4},{6,7},{7,6},{8,9},{9,8},{10,11... | collective-permute-start | bytes 2211848 | tf_op jit(solution)/shard_map/ppermute | solution.py:15
  35.1 2.2 %collective-permute-start.2 = (bf16[96,3584]{1,0:T(8,128)(2,1)S(1)}, bf16[96,3584]{1,0:T(8,128)(2,1)S(1)}, u32[]{:S(2)}, u32[]{:S(2)}) collective-permute-start(bf16[96,3584]{1,0:T(8,128)(2,1)S(1)} %get-tuple-element.10), channel_id=1, source_target_pairs={{0,1},{1,0},{2,3},{3,2},{4,5},{5,4},{6,7},{7,6},{8,9},{9,8},{10,11... | collective-permute-start | bytes 2064392 | tf_op jit(solution)/shard_map/ppermute | solution.py:15
  51.9 7.0 %collective-permute-start.3 = (bf16[6,3584]{1,0:T(8,128)(2,1)S(1)}, bf16[6,3584]{1,0:T(8,128)(2,1)S(1)}, u32[]{:S(2)}, u32[]{:S(2)}) collective-permute-start(bf16[6,3584]{1,0:T(8,128)(2,1)S(1)} %get-tuple-element.12), channel_id=1, source_target_pairs={{0,16},{1,17},{2,18},{3,19},{4,20},{5,21},{6,22},{7,23},{8,24},{9,... | collective-permute-start | bytes 129032 | tf_op jit(solution)/shard_map/ppermute | solution.py:15

commit v2 on v1

--- a/solution.py
+++ b/solution.py
@@ -1,3 +1,5 @@
+import math
+
 import jax
 import jax.numpy as jnp
 from jax import lax
@@ -6,7 +8,8 @@
 from jax.sharding import PartitionSpec as P
 
 VMEM = pl.BlockSpec(memory_space=pltpu.VMEM)
-SMEM = pl.BlockSpec(memory_space=pltpu.SMEM)
+ANY = pl.BlockSpec(memory_space=pl.ANY)
+HBM = pl.BlockSpec(memory_space=pltpu.HBM)
 MIB = 1024 * 1024
 
 
@@ -19,20 +22,34 @@
     return -(-count // 128) * 128
 
 
-def call(kernel, outs, limit, *args, specs=None, flops=0):
-    moved = sum(a.size * a.dtype.itemsize for a in (*args, *outs))
+def call(kernel, outs, limit, *args, specs=None, flops=0, scratch=()):
+    moved = sum(math.prod(a.shape) * a.dtype.itemsize for a in (*args, *outs))
     single = len(outs) == 1
     return pl.pallas_call(
         kernel,
         out_shape=outs[0] if single else tuple(outs),
         in_specs=specs or [VMEM] * len(args),
         out_specs=VMEM if single else tuple([VMEM] * len(outs)),
+        scratch_shapes=list(scratch),
         compiler_params=pltpu.CompilerParams(vmem_limit_bytes=limit),
         cost_estimate=pl.CostEstimate(flops=flops, bytes_accessed=moved, transcendentals=0),
     )(*args)
 
 
-def pack_kernel(draft_ref, states_ref, gain_ref, scores_ref, routes_ref, out_ref):
+def pack_kernel(
+    draft_hbm, states_hbm, gain_hbm, scores_hbm, routes_hbm, out_ref,
+    draft_ref, states_ref, gain_ref, scores_ref, routes_ref, sems,
+):
+    sources = (draft_hbm, states_hbm, gain_hbm, scores_hbm, routes_hbm)
+    targets = (draft_ref, states_ref, gain_ref, scores_ref, routes_ref)
+    copies = [
+        pltpu.make_async_copy(source, target, sems.at[i])
+        for i, (source, target) in enumerate(zip(sources, targets))
+    ]
+    for copy in copies:
+        copy.start()
+    for copy in copies:
+        copy.wait()
     tokens, width = states_ref.shape
     half = width // 2
     extra = out_ref.shape[2] - half
@@ -40,7 +57,7 @@
     slots = tokens // requests
     wide = states_ref[...].astype(jnp.float32)
     mean_square = jnp.mean(wide * wide, axis=-1, keepdims=True)
-    normed = (wide * lax.rsqrt(mean_square + 1e-06) * gain_ref[...]).astype(jnp.bfloat16)
+    normed = (wide * lax.rsqrt(mean_square + 1e-06) * gain_ref[...].reshape(1, width)).astype(jnp.bfloat16)
     scores = scores_ref[...]
     weights = 2.5 * scores / jnp.sum(scores, axis=-1, keepdims=True)
     row = lax.broadcasted_iota(jnp.int32, (tokens, 1), 0)
@@ -61,31 +78,42 @@
     out_ref[1, :, half:] = fine
 
 
-def spread_kernel(own_ref, other_ref, out_ref):
+def load_kernel(*refs):
+    count = (len(refs) - 2) // 2
+    token_ref, sems = refs[-2:]
+    token_ref[...] = jnp.zeros_like(token_ref)
+    copies = [
+        pltpu.make_async_copy(refs[i], refs[count + i], sems.at[i]) for i in range(count)
+    ]
+    for copy in copies:
+        copy.start()
+    for copy in copies:
+        copy.wait()
+
+
+def spread_kernel(own_ref, other_ref, after_ref, out_ref):
     pieces = [own_ref[0], other_ref[0], own_ref[1], other_ref[1]]
     rows = jnp.concatenate([p.astype(jnp.float32) for p in pieces], axis=0).astype(jnp.bfloat16)
     for j in range(out_ref.shape[0]):
         out_ref[j] = rows
 
 
-def expert_kernel(
-    expert_ref, own_ref, other_ref, gate_ref, up_ref, down_ref, keep_ref, give_ref
-):
+def hidden_rows(rows_ref, gate_ref, up_ref):
     half = gate_ref.shape[1] // 2
-    count = own_ref.shape[1] // 2
-    rows = own_ref.shape[0] * count
+    count = rows_ref.shape[1] // 2
 
     def gathered(part):
-        pieces = []
-        for ref in (own_ref, other_ref):
-            for j in range(ref.shape[0]):
-                pieces.append(ref[j, part * count : (part + 1) * count, :].astype(jnp.float32))
+        pieces = [
+            rows_ref[j, part * count : (part + 1) * count, :].astype(jnp.float32)
+            for j in range(rows_ref.shape[0])
+        ]
         return jnp.concatenate(pieces, axis=0)
 
     low, high = gathered(0), gathered(1)
     mixed = low[:, half:] + high[:, half:]
     lane = lax.broadcasted_iota(jnp.int32, mixed.shape, 1)
-    coefficient = jnp.sum(jnp.where(lane == expert_ref[0], mixed, 0.0), axis=1, keepdims=True)
+    expert = lax.axis_index("ep") // 2
+    coefficient = jnp.sum(jnp.where(lane == expert, mixed, 0.0), axis=1, keepdims=True)
     low = low[:, :half].astype(jnp.bfloat16)
     high = high[:, :half].astype(jnp.bfloat16)
 
@@ -95,24 +123,45 @@
 
     gate = projected(gate_ref)
     up = projected(up_ref)
-    hidden = (gate / (1.0 + jnp.exp(-gate)) * up).astype(jnp.bfloat16)
-    step = down_ref.shape[2] // 7
-    for start in range(0, down_ref.shape[2], step):
-        columns = slice(start, start + step)
-        partial = jnp.dot(hidden, down_ref[0, :, columns], preferred_element_type=jnp.float32)
-        partial = partial * coefficient
-        keep_ref[:, columns] = partial[:rows]
-        give_ref[:, columns] = partial[rows:].astype(jnp.bfloat16)
-
-
-def fold_kernel(keep_ref, other_ref, out_ref):
+    return (gate / (1.0 + jnp.exp(-gate)) * up).astype(jnp.bfloat16), coefficient
+
+
+def lowered(hidden, coefficient, down_ref, out_ref, first):
+    step = out_ref.shape[1] // 7
+    for start in range(0, out_ref.shape[1], step):
+        columns = down_ref[0, :, first + start : first + start + step]
+        partial = jnp.dot(hidden, columns, preferred_element_type=jnp.float32)
+        out_ref[:, start : start + step] = (partial * coefficient).astype(out_ref.dtype)
+
+
+def own_kernel(rows_ref, gate_ref, up_ref, down_ref, keep_ref):
+    hidden, coefficient = hidden_rows(rows_ref, gate_ref, up_ref)
+    lowered(hidden, coefficient, down_ref, keep_ref, 0)
+
+
+def low_kernel(
+    rows_ref, gate_ref, up_ref, down_ref, after_ref, give_ref, hidden_ref, coefficient_ref
+):
+    hidden, coefficient = hidden_rows(rows_ref, gate_ref, up_ref)
+    hidden_ref[...] = hidden
+    coefficient_ref[...] = jnp.broadcast_to(coefficient, coefficient_ref.shape)
+    lowered(hidden, coefficient, down_ref, give_ref, 0)
+
+
+def high_kernel(hidden_ref, coefficient_ref, down_ref, give_ref):
+    lowered(
+        hidden_ref[...], coefficient_ref[:, :1], down_ref, give_ref, give_ref.shape[1]
+    )
+
+
+def fold_kernel(keep_ref, low_ref, high_ref, out_ref):
     half = keep_ref.shape[1] // 2
     count = out_ref.shape[1] // 2
     for j in range(out_ref.shape[0]):
         rows = slice(j * count, (j + 1) * count)
-        total = keep_ref[rows, :] + other_ref[rows, :].astype(jnp.float32)
-        both = jnp.concatenate([total[:, :half], total[:, half:]], axis=0)
-        out_ref[j] = both.astype(jnp.bfloat16)
+        low = keep_ref[rows, :half] + low_ref[rows, :].astype(jnp.float32)
+        high = keep_ref[rows, half:] + high_ref[rows, :].astype(jnp.float32)
+        out_ref[j] = jnp.concatenate([low, high], axis=0).astype(jnp.bfloat16)
 
 
 def sum_kernel(parts_ref, keep_ref, give_ref):
@@ -143,23 +192,38 @@
     carried = half + lane_round(devices // 2)
     shape = jax.ShapeDtypeStruct
     bf16, f32 = jnp.bfloat16, jnp.float32
+    small = [
+        pltpu.with_memory_space_constraint(a, pltpu.HBM)
+        for a in (draft_counts, hidden_states, norm_gain, gate_scores, routes)
+    ]
     packed = call(
         pack_kernel,
         [shape((2, tokens, carried), bf16)],
         2 * MIB,
-        draft_counts,
-        hidden_states,
-        norm_gain.reshape(1, width),
-        gate_scores,
-        routes,
-        specs=[SMEM] + [VMEM] * 4,
-    )
+        *small,
+        specs=[HBM] * 5,
+        scratch=[pltpu.SMEM(draft_counts.shape, jnp.int32)]
+        + [pltpu.VMEM(a.shape, a.dtype) for a in small[1:]]
+        + [pltpu.SemaphoreType.DMA((5,))],
+    )
+    weights = (w_gate, w_up, w_down)
+    *loaded, token = call(
+        load_kernel,
+        [pltpu.VMEM(w.shape, w.dtype) for w in weights] + [shape((8, 128), f32)],
+        MIB,
+        *[pltpu.with_memory_space_constraint(w, pltpu.HBM) for w in weights],
+        specs=[HBM] * 3,
+        scratch=[pltpu.SemaphoreType.DMA((3,))],
+    )
+    loaded = [pltpu.with_memory_space_constraint(w, pltpu.VMEM) for w in loaded]
     spread = call(
         spread_kernel,
         [shape((members, 4 * tokens, carried), bf16)],
         8 * MIB,
         packed,
         swapped(packed, far),
+        token,
+        specs=[VMEM, VMEM, ANY],
     )
 
     def exchanged(array):
@@ -170,26 +234,46 @@
     own = exchanged(spread)
     other = swapped(own, 1)
     rows = members * 2 * tokens
-    expert = (lax.axis_index("ep") // 2).astype(jnp.int32).reshape(1)
-    keep, give = call(
-        expert_kernel,
-        [shape((rows, width), f32), shape((rows, width), bf16)],
-        48 * MIB,
-        expert,
+    work = rows * width * w_gate.shape[2]
+    keep = call(
+        own_kernel,
+        [shape((rows, width), f32)],
+        16 * MIB,
         own,
+        *loaded,
+        flops=6 * work,
+    )
+    low, hidden, coefficient = call(
+        low_kernel,
+        [
+            shape((rows, half), bf16),
+            shape((rows, w_gate.shape[2]), bf16),
+            shape((rows, 128), f32),
+        ],
+        16 * MIB,
         other,
-        w_gate,
-        w_up,
-        w_down,
-        specs=[SMEM] + [VMEM] * 5,
-        flops=12 * rows * width * w_gate.shape[2],
+        *loaded,
+        keep,
+        specs=[VMEM] * 4 + [ANY],
+        flops=5 * work,
+    )
+    low = swapped(low, 1)
+    high = call(
+        high_kernel,
+        [shape((rows, half), bf16)],
+        8 * MIB,
+        hidden,
+        coefficient,
+        loaded[2],
+        flops=work,
     )
     folded = call(
         fold_kernel,
         [shape((members, 4 * tokens, half), bf16)],
-        20 * MIB,
+        8 * MIB,
         keep,
-        swapped(give, 1),
+        low,
+        swapped(high, 1),
     )
     keep, give = call(
         sum_kernel,

time: 60 us -> 53.2 us (0.89)
  waiting for transfers between devices: 9.86 us -> 5.68 us
  local copies, waits for them, and re-layouts: 3.57 us -> 0 us
  starting transfers between devices: 8.6 us -> 6.51 us
  Pallas kernels: 8.38 us -> 10.4 us
  blocking collectives: 29.2 us -> 30.4 us
    ppermute x4 -> x5, waiting for transfers between devices: 9.86 us -> 5.68 us  [swapped(): return lax.ppermute(array, 'ep', [(i, i ^ distance) for i in range(size)])]
    unnamed x8 -> x0, local copies, waits for them, and re-layouts: 2.84 us -> none
    ppermute x4 -> x5, starting transfers between devices: 8.6 us -> 6.51 us  [swapped(): return lax.ppermute(array, 'ep', [(i, i ^ distance) for i in range(size)])]
    pallas_call x6 -> x9, Pallas kernels: 8.38 us -> 10.4 us  [call(): pl.pallas_call(kernel, out_shape=outs[0] if single else tuple(outs), in_s...]
    all_to_all x2, blocking collectives: 29.2 us -> 30.4 us  [exchanged(): lax.all_to_all(array, 'ep', split_axis=0, concat_axis=0, axis_index_group...]
    reshape x1 -> x0, local copies, waits for them, and re-layouts: 0.73 us -> none  [body(): norm_gain.reshape(1, width)]
  transfers between devices with their start and end apart: 4 -> 5, of which waited for: 4 -> 4; matrix products, arithmetic and copies ran while one was open for 0% -> 0% of each run, Pallas kernels for 0% -> 12%
where the time goes in v2:
time: 53.2 us; the launch traced here: 53 us
  blocking collectives  30.4 us (57%)
  Pallas kernels  10.4 us (20%)
  starting transfers between devices  6.51 us (12%)
  waiting for transfers between devices  5.68 us (11%)
    all_to_all x2, blocking collectives, exchanged(): lax.all_to_all(array, 'ep', split_axis=0, concat_axis=0, axis_index_group...  30.4 us
    pallas_call x9, Pallas kernels, call(): pl.pallas_call(kernel, out_shape=outs[0] if single else tuple(outs), in_s...  10.4 us
    ppermute x5, starting transfers between devices, swapped(): return lax.ppermute(array, 'ep', [(i, i ^ distance) for i in range(size)])  6.51 us
    ppermute x5, waiting for transfers between devices, swapped(): return lax.ppermute(array, 'ep', [(i, i ^ distance) for i in range(size)])  5.68 us
  transfers between devices with their start and end apart: 5, of which 4 were waited for; matrix products, arithmetic and copies ran while one was open for 0% of the time, Pallas kernels for 12%

profile of v2, /device:TPU:0, one launch (start us, length us, event | category | flops | bytes accessed | tf_op | source)
XLA Modules:
  0.0 53.0 jit_solution(12572397232569647723)
XLA Ops:
  0.0 1.1 %shard_map.82.own_ref = bf16[2,6,1920]{2,1,0:T(8,128)(2,1)S(1)} custom-call(s32[2]{0:T(128)} %draft_hbm.1, bf16[6,3584]{1,0:T(8,128)(2,1)} %states_hbm.1, f32[3584]{0:T(1024)} %gain_hbm.1, f32[6,8]{1,0:T(8,128)} %scores_hbm.1, s32[6,8]{1,0:T(8,128)} %routes_hbm.1), custom_call_target="tpu_custom_call" | custom-call | bytes 103816 | tf_op jit(solution)/shard_map/pallas_call | solution.py:28
  1.1 4.1 %collective-permute-start = (bf16[2,6,1920]{2,1,0:T(8,128)(2,1)S(1)}, bf16[2,6,1920]{2,1,0:T(8,128)(2,1)S(1)}, u32[]{:S(2)}, u32[]{:S(2)}) collective-permute-start(bf16[2,6,1920]{2,1,0:T(8,128)(2,1)S(1)} %shard_map.82.own_ref), channel_id=1, source_target_pairs={{0,16},{1,17},{2,18},{3,19},{4,20},{5,21},{6,22},{7,23},{8,24},{9,... | collective-permute-start | bytes 138248 | tf_op jit(solution)/shard_map/ppermute | solution.py:18
  5.2 4.2 %shard_map.83 = (bf16[1,3584,512]{2,1,0:T(8,128)(2,1)S(1)}, bf16[1,3584,512]{2,1,0:T(8,128)(2,1)S(1)}, bf16[1,512,3584]{2,1,0:T(8,128)(2,1)S(1)}, f32[8,128]{1,0:T(8,128)S(1)}) custom-call(bf16[1,3584,512]{2,1,0:T(8,128)(2,1)} %refs_0_.1, bf16[1,3584,512]{2,1,0:T(8,128)(2,1)} %refs_1_.1, bf16[1,512,3584]{2,1,0:T(8,128)(2,1)} %refs_2_.1), custom_call_target="tpu_custom_call" | custom-call | bytes 22024192 | tf_op jit(solution)/shard_map/pallas_call | solution.py:28
  9.4 0.0 collective-permute-done.other_ref
  9.4 0.1 shard_map.84
  9.5 16.0 %all_to_all.10.rows_ref = bf16[8,24,1920]{2,1,0:T(8,128)(2,1)S(1)} all-to-all(bf16[8,24,1920]{2,1,0:T(8,128)(2,1)S(1)} %shard_map.84), channel_id=1, replica_groups={{0,2,4,6,8,10,12,14},{1,3,5,7,9,11,13,15},{16,18,20,22,24,26,28,30},{17..., dimensions={0} | all-to-all | bytes 1474560 | tf_op jit(solution)/shard_map/all_to_all | solution.py:230
  25.5 0.0 collective-permute-start.1
  25.5 2.0 %shard_map.85.after_ref.keep_ref = f32[96,3584]{1,0:T(8,128)S(1)} custom-call(bf16[8,24,1920]{2,1,0:T(8,128)(2,1)S(1)} %all_to_all.10.rows_ref, bf16[1,3584,512]{2,1,0:T(8,128)(2,1)S(1)} %get-tuple-element.15.gate_ref, bf16[1,3584,512]{2,1,0:T(8,128)(2,1)S(1)} %get-tuple-element.16.up_ref, bf16[1,512,3584]{2,1,0:T(8,128)(2,1)S(1)} %get-tuple-element.17.down_ref), custom_call_target="tpu_custom_call" | custom-call | flops 1056964608 | bytes 13123584 | tf_op jit(solution)/shard_map/pallas_call | solution.py:28
  27.5 0.2 collective-permute-done.1.rows_ref
  27.7 1.7 %shard_map.86 = (bf16[96,1792]{1,0:T(8,128)(2,1)S(1)}, bf16[96,512]{1,0:T(8,128)(2,1)S(1)}, f32[96,128]{1,0:T(8,128)S(1)}) custom-call(bf16[8,24,1920]{2,1,0:T(8,128)(2,1)S(1)} %collective-permute-done.1.rows_ref, bf16[1,3584,512]{2,1,0:T(8,128)(2,1)S(1)} %get-tuple-element.15.gate_ref, bf16[1,3584,512]{2,1,0:T(8,128)(2,1)S(1)} %get-tuple-element.16.up_ref, ...), custom_call_target="tpu_custom_call" | custom-call | flops 880803840 | bytes 13615104 | tf_op jit(solution)/shard_map/pallas_call | solution.py:28
  29.4 0.3 collective-permute-start.2
  29.8 0.4 shard_map.87
  30.2 0.3 collective-permute-start.3
  30.5 0.6 %collective-permute-done.2.low_ref = bf16[96,1792]{1,0:T(8,128)(2,1)S(1)} collective-permute-done((bf16[96,1792]{1,0:T(8,128)(2,1)S(1)}, bf16[96,1792]{1,0:T(8,128)(2,1)S(1)}, u32[]{:S(2)}, u32[]{:S(2)}) %collective-permute-start.2) | collective-permute-done | bytes 344096 | tf_op jit(solution)/shard_map/ppermute | solution.py:18
  31.1 0.8 %collective-permute-done.3.high_ref = bf16[96,1792]{1,0:T(8,128)(2,1)S(1)} collective-permute-done((bf16[96,1792]{1,0:T(8,128)(2,1)S(1)}, bf16[96,1792]{1,0:T(8,128)(2,1)S(1)}, u32[]{:S(2)}, u32[]{:S(2)}) %collective-permute-start.3) | collective-permute-done | bytes 344096 | tf_op jit(solution)/shard_map/ppermute | solution.py:18
  31.9 0.2 shard_map.88
  32.1 14.4 %all_to_all.11.parts_ref = bf16[8,24,1792]{2,1,0:T(8,128)(2,1)S(1)} all-to-all(bf16[8,24,1792]{2,1,0:T(8,128)(2,1)S(1)} %shard_map.88), channel_id=1, replica_groups={{0,2,4,6,8,10,12,14},{1,3,5,7,9,11,13,15},{16,18,20,22,24,26,28,30},{17..., dimensions={0} | all-to-all | bytes 1376256 | tf_op jit(solution)/shard_map/all_to_all | solution.py:230
  46.5 0.1 shard_map.89
  46.6 1.7 %collective-permute-start.4 = (bf16[6,3584]{1,0:T(8,128)(2,1)S(1)}, bf16[6,3584]{1,0:T(8,128)(2,1)S(1)}, u32[]{:S(2)}, u32[]{:S(2)}) collective-permute-start(bf16[6,3584]{1,0:T(8,128)(2,1)S(1)} %get-tuple-element.22), channel_id=1, source_target_pairs={{0,16},{1,17},{2,18},{3,19},{4,20},{5,21},{6,22},{7,23},{8,24},{9,... | collective-permute-start | bytes 129032 | tf_op jit(solution)/shard_map/ppermute | solution.py:18
  48.4 4.0 %collective-permute-done.4.other_ref = bf16[6,3584]{1,0:T(8,128)(2,1)S(1)} collective-permute-done((bf16[6,3584]{1,0:T(8,128)(2,1)S(1)}, bf16[6,3584]{1,0:T(8,128)(2,1)S(1)}, u32[]{:S(2)}, u32[]{:S(2)}) %collective-permute-start.4) | collective-permute-done | bytes 43040 | tf_op jit(solution)/shard_map/ppermute | solution.py:18
  52.4 0.6 %shard_map.90 = bf16[6,3584]{1,0:T(8,128)(2,1)} custom-call(f32[6,3584]{1,0:T(8,128)S(1)} %get-tuple-element.21.keep_ref, bf16[6,3584]{1,0:T(8,128)(2,1)S(1)} %collective-permute-done.4.other_ref), custom_call_target="tpu_custom_call" | custom-call | bytes 172032 | tf_op jit(solution)/shard_map/pallas_call | solution.py:28
Async XLA Ops:
  1.1 8.4 %collective-permute-start = (bf16[2,6,1920]{2,1,0:T(8,128)(2,1)S(1)}, bf16[2,6,1920]{2,1,0:T(8,128)(2,1)S(1)}, u32[]{:S(2)}, u32[]{:S(2)}) collective-permute-start(bf16[2,6,1920]{2,1,0:T(8,128)(2,1)S(1)} %shard_map.82.own_ref), channel_id=1, source_target_pairs={{0,16},{1,17},{2,18},{3,19},{4,20},{5,21},{6,22},{7,23},{8,24},{9,... | collective-permute-start | bytes 138248 | tf_op jit(solution)/shard_map/ppermute | solution.py:18
  25.5 2.2 %collective-permute-start.1 = (bf16[8,24,1920]{2,1,0:T(8,128)(2,1)S(1)}, bf16[8,24,1920]{2,1,0:T(8,128)(2,1)S(1)}, u32[]{:S(2)}, u32[]{:S(2)}) collective-permute-start(bf16[8,24,1920]{2,1,0:T(8,128)(2,1)S(1)} %all_to_all.10.rows_ref), channel_id=1, source_target_pairs={{0,1},{1,0},{2,3},{3,2},{4,5},{5,4},{6,7},{7,6},{8,9},{9,8},{10,11... | collective-permute-start | bytes 2211848 | tf_op jit(solution)/shard_map/ppermute | solution.py:18
  29.4 1.7 %collective-permute-start.2 = (bf16[96,1792]{1,0:T(8,128)(2,1)S(1)}, bf16[96,1792]{1,0:T(8,128)(2,1)S(1)}, u32[]{:S(2)}, u32[]{:S(2)}) collective-permute-start(bf16[96,1792]{1,0:T(8,128)(2,1)S(1)} %get-tuple-element.18), channel_id=1, source_target_pairs={{0,1},{1,0},{2,3},{3,2},{4,5},{5,4},{6,7},{7,6},{8,9},{9,8},{10,11... | collective-permute-start | bytes 1032200 | tf_op jit(solution)/shard_map/ppermute | solution.py:18
  30.2 1.7 %collective-permute-start.3 = (bf16[96,1792]{1,0:T(8,128)(2,1)S(1)}, bf16[96,1792]{1,0:T(8,128)(2,1)S(1)}, u32[]{:S(2)}, u32[]{:S(2)}) collective-permute-start(bf16[96,1792]{1,0:T(8,128)(2,1)S(1)} %shard_map.87), channel_id=1, source_target_pairs={{0,1},{1,0},{2,3},{3,2},{4,5},{5,4},{6,7},{7,6},{8,9},{9,8},{10,11... | collective-permute-start | bytes 1032200 | tf_op jit(solution)/shard_map/ppermute | solution.py:18
  46.6 5.8 %collective-permute-start.4 = (bf16[6,3584]{1,0:T(8,128)(2,1)S(1)}, bf16[6,3584]{1,0:T(8,128)(2,1)S(1)}, u32[]{:S(2)}, u32[]{:S(2)}) collective-permute-start(bf16[6,3584]{1,0:T(8,128)(2,1)S(1)} %get-tuple-element.22), channel_id=1, source_target_pairs={{0,16},{1,17},{2,18},{3,19},{4,20},{5,21},{6,22},{7,23},{8,24},{9,... | collective-permute-start | bytes 129032 | tf_op jit(solution)/shard_map/ppermute | solution.py:18
